TPU v7x, 512 devices: a whole 4x4x16 slice. The times are simulated.
512 devices in a mesh: mp: 2 (over y_hi), tok: 8 (over x, core), lat: 32 (over z, y_lo).
Axes of the slice: x: 4, y: 4 (y_hi: 2, y_lo: 2; y = y_hi * 2 + y_lo), z: 16, core: 2. Of those that a mesh axis runs over, the one named last changes fastest.
Arguments:
- inputs: bfloat16 [2, 384, 4608], P('mp', 'lat', 'tok'), may hold values from -6 to 6
- gate_w: bfloat16 [2, 4608, 18432], P('mp', 'tok', 'lat'), may hold values from -0.09375 to 0.09375
- up_w: bfloat16 [2, 4608, 18432], P('mp', 'tok', 'lat'), may hold values from -0.09375 to 0.09375
- down_w: bfloat16 [2, 18432, 4608], P('mp', 'lat', 'tok'), may hold values from -0.046875 to 0.046875
- enc_w: bfloat16 [2, 4608, 8192], P('mp', 'tok', 'lat'), may hold values from -0.0625 to 0.0625
- enc_bias: float32 [8192], P('lat'), may hold values from -3 to 3
- dec_w: bfloat16 [8192, 2, 4608], P('lat', 'mp', 'tok'), may hold values from -0.0625 to 0.0625
- dec_bias: float32 [2, 4608], P('mp', 'tok'), may hold values from -3 to 3
Outputs:
- recon_error: float32 [2, 384, 4608], P('mp', 'lat', 'tok')
- dec_grad: float32 [8192, 2, 4608], P('lat', 'mp', 'tok')
- latent_grad: float32 [384, 8192], P(None, 'lat')
All inputs are finite; a program needn't handle non-finite values.
Results may differ from a plain program's by a relative error of at most 0.009.
Values may be sent and summed in bfloat16 or wider, within the bound.
A program may use at most 64 MiB of HBM per device.

v0:
```python
import jax
import jax.numpy as jnp
from jax import lax
from jax.sharding import PartitionSpec as P


def contract_rows(left, right):
    return lax.dot_general(
        left, right, (((0,), (0,)), ((), ())), preferred_element_type=jnp.float32
    )


def contract_cols(left, right):
    return lax.dot_general(
        left, right, (((1,), (1,)), ((), ())), preferred_element_type=jnp.float32
    )


def body(inputs, gate_w, up_w, down_w, enc_w, enc_bias, dec_w, dec_bias):
    x_rows = inputs[0]
    gathered = lax.all_gather(x_rows, "lat", axis=0, tiled=True)
    gate_local = gate_w[0]
    up_local = up_w[0]
    width = gate_local.shape[1]
    block = gathered
    both = lax.psum_scatter(
        jnp.concatenate(
            [
                jnp.dot(block, gate_local, preferred_element_type=jnp.float32),
                jnp.dot(block, up_local, preferred_element_type=jnp.float32),
            ],
            axis=1,
        ),
        "tok",
        scatter_dimension=0,
        tiled=True,
    )
    hidden = (jax.nn.gelu(both[:, :width], approximate=True) * both[:, width:]).astype(jnp.bfloat16)
    hidden_all = lax.all_gather(hidden, "tok", axis=0, tiled=True)
    down_local = down_w[0]
    block = hidden_all
    acts = lax.psum_scatter(
        jnp.dot(block, down_local, preferred_element_type=jnp.float32),
        "lat",
        scatter_dimension=0,
        tiled=True,
    ).astype(jnp.bfloat16)
    acts_all = lax.all_gather(acts, "lat", axis=0, tiled=True)
    partial_pre = jnp.dot(acts_all, enc_w[0], preferred_element_type=jnp.float32)
    pre = lax.psum(partial_pre, ("mp", "tok"))
    codes = jnp.maximum(pre + enc_bias, 0.0).astype(jnp.bfloat16)
    decoder = dec_w[:, 0, :]
    bias_row = dec_bias[0]
    block = codes
    recon = lax.psum_scatter(
        jnp.dot(block, decoder, preferred_element_type=jnp.float32),
        "lat",
        scatter_dimension=0,
        tiled=True,
    )
    error = recon + bias_row - acts.astype(jnp.float32)
    error_all = lax.all_gather(error.astype(jnp.bfloat16), "lat", axis=0, tiled=True)
    decoder_grad = contract_rows(codes, error_all)
    latent_grad = lax.psum(contract_cols(error_all, decoder), ("mp", "tok"))
    return (error[None], decoder_grad[:, None, :], latent_grad)


def solution(mesh):
    in_specs = (
        P("mp", "lat", "tok"),
        P("mp", "tok", "lat"),
        P("mp", "tok", "lat"),
        P("mp", "lat", "tok"),
        P("mp", "tok", "lat"),
        P("lat"),
        P("lat", "mp", "tok"),
        P("mp", "tok"),
    )
    out_specs = (P("mp", "lat", "tok"), P("lat", "mp", "tok"), P(None, "lat"))
    return jax.shard_map(body, mesh=mesh, in_specs=in_specs, out_specs=out_specs, check_vma=False)
```

profile of v0, /device:TPU:1, one launch (start us, length us, event | category | flops | bytes accessed | tf_op | source)
XLA Modules:
  0.0 789.7 jit_solution(4947730989583786598)
XLA Ops:
  7.2 0.0 reduce-scatter.8.cloned.1.call-start
  7.2 0.8 copy.20
  8.0 61.9 %all-gather = bf16[1,384,576]{2,0,1:T(2,128)(2,1)S(1)} all-gather(bf16[1,12,576]{2,0,1:T(2,128)(2,1)S(1)} %copy.20), channel_id=2, replica_groups=mesh['mp'=2,'tok'=8,'lat'=32] {'lat'}, dimensions={1}, use_global_device_ids=true | all-gather | bytes 456192 | tf_op jit(solution)/shard_map/all_gather | solution.py:21
  70.0 0.7 copy.21
  70.6 0.6 fusion.4
  71.3 0.6 fusion.6
  71.9 0.1 pad_maximum_fusion
  72.1 2.0 copy.25
  74.1 0.0 all-reduce.7.cloned.1.call-start
  74.1 47.7 %reduce-scatter.8.cloned.1.call-done = f32[48,1152]{1,0:T(8,128)} async-done(((f32[384,1152]{1,0:T(8,128)}), f32[48,1152]{1,0:T(8,128)}) %reduce-scatter.8.cloned.1.call-update) | async-done | bytes 221200 | tf_op jit(solution)/shard_map/reduce_scatter | solution.py:26
  121.8 1.1 fusion.24
  122.9 15.4 %all_gather.13 = bf16[384,576]{1,0:T(8,128)(2,1)S(1)} all-gather(bf16[48,576]{1,0:T(8,128)(2,1)S(1)} %fusion.24), channel_id=1, replica_groups=mesh['mp'=2,'tok'=8,'lat'=32] {'tok'}, dimensions={0}, use_global_device_ids=true | all-gather | bytes 497664 | tf_op jit(solution)/shard_map/all_gather | solution.py:39
  138.2 0.6 fusion.2
  138.8 59.0 %fusion = f32[16,576]{1,0:T(8,128)S(1)} fusion(f32[384,576]{1,0:T(8,128)S(1)} %fusion.2), kind=kCustom, calls=%all-reduce-scatter | all-reduce-scatter fusion | flops 294913 | bytes 923648
  197.9 1.7 collective-permute-start
  199.6 2.1 collective-permute-start.1
  201.7 6.0 collective-permute-start.7
  207.7 4.9 collective-permute-start.2
  212.7 4.9 collective-permute-start.3
  217.6 2.1 collective-permute-start.4
  219.8 3.5 collective-permute-start.5
  223.2 2.8 collective-permute-start.6
  226.1 1.3 dynamic-slice.6
  228.1 1.3 concatenate.4
  229.4 49.4 %all-gather.1 = bf16[32,12,576]{2,1,0:T(8,128)(2,1)S(1)} all-gather(bf16[1,12,576]{2,1,0:T(8,128)(2,1)S(1)} %fusion.31), channel_id=1, replica_groups=mesh['mp'=2,'tok'=8,'lat'=32] {'lat'}, dimensions={0}, use_global_device_ids=true | all-gather | bytes 456192 | tf_op jit(solution)/shard_map/all_gather | solution.py:48
  278.8 0.2 reshape.9
  279.1 1.1 fusion.14
  280.2 0.0 all-reduce.9.cloned.1.call-start
  280.2 180.0 %all-reduce.7.cloned.1.call-done = f32[384,256]{1,0:T(8,128)} async-done(((f32[384,256]{1,0:T(8,128)}), f32[384,256]{1,0:T(8,128)}) %all-reduce.7.cloned.1.call-update) | async-done | bytes 393232 | tf_op jit(solution)/shard_map/psum | solution.py:50
  460.2 1.3 fusion.12
  461.6 59.2 %fusion.1 = f32[16,576]{1,0:T(8,128)S(1)} fusion(f32[384,576]{1,0:T(8,128)S(1)} %fusion.12), kind=kCustom, calls=%all-reduce-scatter.1 | all-reduce-scatter fusion | flops 294913 | bytes 923648
  520.7 1.3 collective-permute-start.10
  522.0 3.4 collective-permute-start.11
  525.5 7.0 collective-permute-start.15
  532.6 4.5 collective-permute-start.12
  537.1 3.9 collective-permute-start.13
  541.0 2.9 collective-permute-start.14
  543.9 3.1 collective-permute-start.8
  547.0 2.2 collective-permute-start.9
  549.3 1.0 collective-permute-done.9
  550.3 1.0 concatenate.5
  551.3 48.9 %all-gather.2 = bf16[32,12,576]{2,1,0:T(8,128)(2,1)S(1)} all-gather(bf16[1,12,576]{2,1,0:T(8,128)(2,1)S(1)} %get-tuple-element.18), channel_id=1, replica_groups=mesh['mp'=2,'tok'=8,'lat'=32] {'lat'}, dimensions={0}, use_global_device_ids=true | all-gather | bytes 456192 | tf_op jit(solution)/shard_map/all_gather | solution.py:62
  600.2 0.2 reshape.11
  600.4 1.1 fusion.10
  601.5 0.6 copy.24
  602.2 1.2 convolution_bitcast_fusion
  603.3 178.1 %all-reduce.9.cloned.1.call-done = f32[384,256]{1,0:T(8,128)} async-done(((f32[384,256]{1,0:T(8,128)}), f32[384,256]{1,0:T(8,128)}) %all-reduce.9.cloned.1.call-update) | async-done | bytes 393232 | tf_op jit(solution)/shard_map/psum | solution.py:64
  781.4 1.8 copy.29
  (40 shorter events, 0.2 us)
Async XLA Ops:
  7.2 63.5 %copy-start = (bf16[1,576,576]{2,1,0:T(8,128)(2,1)S(1)}, bf16[1,576,576]{2,1,0:T(8,128)(2,1)}, u32[]{:S(2)}) copy-start(bf16[1,576,576]{2,1,0:T(8,128)(2,1)} %param.10) | copy-start | bytes 1990660
  7.2 114.6 %reduce-scatter.8.cloned.1.call-start = ((), (), s32[]{:S(2)}) async-start(), calls=%async_computation.3 | async-start | bytes 1990656 | tf_op jit(solution)/shard_map/reduce_scatter | solution.py:26
  70.0 1.3 copy-start.3
  74.0 64.2 %copy-start.4 = (bf16[1,576,576]{2,1,0:T(8,128)(2,1)S(1)}, bf16[1,576,576]{2,1,0:T(8,128)(2,1)}, u32[]{:S(2)}) copy-start(bf16[1,576,576]{2,1,0:T(8,128)(2,1)} %param.11) | copy-start | bytes 1990660
  74.1 386.2 %all-reduce.7.cloned.1.call-start = ((), (), s32[]{:S(2)}) async-start(), calls=%async_computation.1 | async-start | bytes 786432 | tf_op jit(solution)/shard_map/psum | solution.py:50
  138.8 140.3 %copy-start.5 = (bf16[1,576,256]{2,1,0:T(8,128)(2,1)S(1)}, bf16[1,576,256]{2,1,0:T(8,128)(2,1)}, u32[]{:S(2)}) copy-start(bf16[1,576,256]{2,1,0:T(8,128)(2,1)} %param.12) | copy-start | bytes 884740
  197.9 21.9 %collective-permute-start = (bf16[16,576]{1,0:T(8,128)(2,1)S(1)}, bf16[16,576]{1,0:T(8,128)(2,1)S(1)}, u32[]{:S(2)}, u32[]{:S(2)}) collective-permute-start(bf16[16,576]{1,0:T(8,128)(2,1)S(1)} %convert.14), channel_id=1, source_target_pairs={{0,1},{1,2},{2,3},{3,4},{4,5},{5,6},{6,7},{7,8},{8,9},{9,10},{10,1... | collective-permute-start | bytes 55304
  199.6 23.6 %collective-permute-start.1 = (bf16[16,576]{1,0:T(8,128)(2,1)S(1)}, bf16[16,576]{1,0:T(8,128)(2,1)S(1)}, u32[]{:S(2)}, u32[]{:S(2)}) collective-permute-start(bf16[16,576]{1,0:T(8,128)(2,1)S(1)} %convert.14), channel_id=1, source_target_pairs={{0,2},{1,3},{2,4},{3,5},{4,6},{5,7},{6,8},{7,9},{8,10},{9,11},{10,... | collective-permute-start | bytes 55304
  201.7 15.9 %collective-permute-start.7 = (bf16[12,576]{1,0:T(8,128)(2,1)S(1)}, bf16[12,576]{1,0:T(8,128)(2,1)S(1)}, u32[]{:S(2)}, u32[]{:S(2)}) collective-permute-start(bf16[12,576]{1,0:T(8,128)(2,1)S(1)} %slice.10), channel_id=1, source_target_pairs={{0,8},{1,9},{2,10},{3,11},{4,12},{5,13},{6,14},{7,15},{8,16},{9,17... | collective-permute-start | bytes 41480
  207.7 20.3 %collective-permute-start.2 = (bf16[16,576]{1,0:T(8,128)(2,1)S(1)}, bf16[16,576]{1,0:T(8,128)(2,1)S(1)}, u32[]{:S(2)}, u32[]{:S(2)}) collective-permute-start(bf16[16,576]{1,0:T(8,128)(2,1)S(1)} %convert.14), channel_id=1, source_target_pairs={{0,3},{1,4},{2,5},{3,6},{4,7},{5,8},{6,9},{7,10},{8,11},{9,12},{10... | collective-permute-start | bytes 55304
  212.7 15.3 %collective-permute-start.3 = (bf16[16,576]{1,0:T(8,128)(2,1)S(1)}, bf16[16,576]{1,0:T(8,128)(2,1)S(1)}, u32[]{:S(2)}, u32[]{:S(2)}) collective-permute-start(bf16[16,576]{1,0:T(8,128)(2,1)S(1)} %convert.14), channel_id=1, source_target_pairs={{0,4},{1,5},{2,6},{3,7},{4,8},{5,9},{6,10},{7,11},{8,12},{9,13},{1... | collective-permute-start | bytes 55304
  217.6 10.4 %collective-permute-start.4 = (bf16[16,576]{1,0:T(8,128)(2,1)S(1)}, bf16[16,576]{1,0:T(8,128)(2,1)S(1)}, u32[]{:S(2)}, u32[]{:S(2)}) collective-permute-start(bf16[16,576]{1,0:T(8,128)(2,1)S(1)} %convert.14), channel_id=1, source_target_pairs={{0,5},{1,6},{2,7},{3,8},{4,9},{5,10},{6,11},{7,12},{8,13},{9,14},{... | collective-permute-start | bytes 55304
  219.8 8.3 %collective-permute-start.5 = (bf16[16,576]{1,0:T(8,128)(2,1)S(1)}, bf16[16,576]{1,0:T(8,128)(2,1)S(1)}, u32[]{:S(2)}, u32[]{:S(2)}) collective-permute-start(bf16[16,576]{1,0:T(8,128)(2,1)S(1)} %convert.14), channel_id=1, source_target_pairs={{0,6},{1,7},{2,8},{3,9},{4,10},{5,11},{6,12},{7,13},{8,14},{9,15},... | collective-permute-start | bytes 55304
  223.2 4.8 collective-permute-start.6
  229.4 230.8 %copy-start.2 = (bf16[256,1,576]{0,2,1:T(8,128)(2,1)S(1)}, bf16[256,1,576]{0,2,1:T(8,128)(2,1)}, u32[]{:S(2)}) copy-start(bf16[256,1,576]{0,2,1:T(8,128)(2,1)} %param.14) | copy-start | bytes 884740
  229.4 230.8 %copy-start.6 = (f32[256]{0:T(256)S(1)}, f32[256]{0:T(256)}, u32[]{:S(2)}) copy-start(f32[256]{0:T(256)} %param.13) | copy-start | bytes 3076
  280.2 269.0 %copy-start.7 = (f32[1,576]{1,0:T(1,128)S(1)}, f32[1,576]{1,0:T(1,128)}, u32[]{:S(2)}) copy-start(f32[1,576]{1,0:T(1,128)} %param.15) | copy-start | bytes 6916
  280.2 501.2 %all-reduce.9.cloned.1.call-start = ((), (), s32[]{:S(2)}) async-start(), calls=%async_computation.2 | async-start | bytes 786432 | tf_op jit(solution)/shard_map/psum | solution.py:64
  520.7 23.1 %collective-permute-start.10 = (f32[16,576]{1,0:T(8,128)S(1)}, f32[16,576]{1,0:T(8,128)S(1)}, u32[]{:S(2)}, u32[]{:S(2)}) collective-permute-start(f32[16,576]{1,0:T(8,128)S(1)} %fusion.1), channel_id=1, source_target_pairs={{0,3},{1,4},{2,5},{3,6},{4,7},{5,8},{6,9},{7,10},{8,11},{9,12},{10... | collective-permute-start | bytes 110600
  522.0 24.9 %collective-permute-start.11 = (f32[16,576]{1,0:T(8,128)S(1)}, f32[16,576]{1,0:T(8,128)S(1)}, u32[]{:S(2)}, u32[]{:S(2)}) collective-permute-start(f32[16,576]{1,0:T(8,128)S(1)} %fusion.1), channel_id=1, source_target_pairs={{0,4},{1,5},{2,6},{3,7},{4,8},{5,9},{6,10},{7,11},{8,12},{9,13},{1... | collective-permute-start | bytes 110600
  525.5 15.5 %collective-permute-start.15 = (f32[12,576]{1,0:T(8,128)S(1)}, f32[12,576]{1,0:T(8,128)S(1)}, u32[]{:S(2)}, u32[]{:S(2)}) collective-permute-start(f32[12,576]{1,0:T(8,128)S(1)} %slice.11), channel_id=1, source_target_pairs={{0,8},{1,9},{2,10},{3,11},{4,12},{5,13},{6,14},{7,15},{8,16},{9,17... | collective-permute-start | bytes 82952
  532.6 16.7 %collective-permute-start.12 = (f32[16,576]{1,0:T(8,128)S(1)}, f32[16,576]{1,0:T(8,128)S(1)}, u32[]{:S(2)}, u32[]{:S(2)}) collective-permute-start(f32[16,576]{1,0:T(8,128)S(1)} %fusion.1), channel_id=1, source_target_pairs={{0,5},{1,6},{2,7},{3,8},{4,9},{5,10},{6,11},{7,12},{8,13},{9,14},{... | collective-permute-start | bytes 110600
  537.1 12.2 %collective-permute-start.13 = (f32[16,576]{1,0:T(8,128)S(1)}, f32[16,576]{1,0:T(8,128)S(1)}, u32[]{:S(2)}, u32[]{:S(2)}) collective-permute-start(f32[16,576]{1,0:T(8,128)S(1)} %fusion.1), channel_id=1, source_target_pairs={{0,6},{1,7},{2,8},{3,9},{4,10},{5,11},{6,12},{7,13},{8,14},{9,15},... | collective-permute-start | bytes 110600
  541.0 8.2 %collective-permute-start.14 = (f32[16,576]{1,0:T(8,128)S(1)}, f32[16,576]{1,0:T(8,128)S(1)}, u32[]{:S(2)}, u32[]{:S(2)}) collective-permute-start(f32[16,576]{1,0:T(8,128)S(1)} %fusion.1), channel_id=1, source_target_pairs={{0,7},{1,8},{2,9},{3,10},{4,11},{5,12},{6,13},{7,14},{8,15},{9,16}... | collective-permute-start | bytes 110600
  543.9 5.4 collective-permute-start.8
  547.0 3.3 collective-permute-start.9
  551.3 50.8 %copy-start.1 = (f32[384,256]{1,0:T(8,128)S(1)}, f32[384,256]{1,0:T(8,128)}, u32[]{:S(2)}) copy-start(f32[384,256]{1,0:T(8,128)} %all-reduce.7.cloned.1.call-done) | copy-start | bytes 1179652
Sparse Core Ops, SparseCore 0:
  74.2 47.5 reduce-scatter.7
  280.3 179.8 all-reduce.6
  601.6 179.7 all-reduce.8
where the time goes:
time: 790 us
  waiting for transfers between devices  407 us (52%)
  blocking collectives  294 us (37%)
  starting transfers between devices  56.6 us (7%)
  between operations  14.9 us (2%)
  local copies, waits for them, and re-layouts  10 us (1%)
    psum x1, waiting for transfers between devices, body(): pre = lax.psum(partial_pre, ('mp', 'tok'))  180 us
    psum x1, waiting for transfers between devices, body(): latent_grad = lax.psum(contract_cols(error_all, decoder), ('mp', 'tok'))  178 us
    unnamed x2, blocking collectives  118 us
    all_gather x1, blocking collectives, body(): gathered = lax.all_gather(x_rows, 'lat', axis=0, tiled=True)  61.9 us
    unnamed x16, starting transfers between devices  56.5 us
    all_gather x1, blocking collectives, body(): acts_all = lax.all_gather(acts, 'lat', axis=0, tiled=True)  49.4 us
    all_gather x1, blocking collectives, body(): lax.all_gather(error.astype(jnp.bfloat16), 'lat', axis=0, tiled=True)  48.9 us
    reduce_scatter x1, waiting for transfers between devices, body(): lax.psum_scatter(jnp.concatenate([jnp.dot(block, gate_local, preferred_el...  47.7 us
  transfers between devices with their start and end apart: 19, of which 4 were waited for; matrix products, arithmetic and copies ran while one was open for 0% of the time, Pallas kernels for 0%

commit v1 on v0

--- a/solution.py
+++ b/solution.py
@@ -59,7 +59,16 @@
         tiled=True,
     )
     error = recon + bias_row - acts.astype(jnp.float32)
-    error_all = lax.all_gather(error.astype(jnp.bfloat16), "lat", axis=0, tiled=True)
+    unit = error.astype(jnp.bfloat16)
+    error_all = jnp.concatenate(
+        lax.all_to_all(
+            jnp.stack([unit for _ in range(lax.axis_size("lat"))]),
+            axis_name="lat",
+            split_axis=0,
+            concat_axis=0,
+        ),
+        axis=0,
+    )
     decoder_grad = contract_rows(codes, error_all)
     latent_grad = lax.psum(contract_cols(error_all, decoder), ("mp", "tok"))
     return (error[None], decoder_grad[:, None, :], latent_grad)

time: 790 us -> 759 us (0.961)
  blocking collectives: 294 us -> 277 us
  waiting for transfers between devices: 407 us -> 392 us
    all_gather x1 -> x0, blocking collectives: 48.9 us -> none  [body(): lax.all_gather(error.astype(jnp.bfloat16), 'lat', axis=0, tiled=True)]
    all_to_all x0 -> x1, blocking collectives: none -> 32.4 us  [body(): lax.all_to_all(jnp.stack([unit for _ in range(lax.axis_size('lat'))]), ax...]
    psum x1, waiting for transfers between devices: 178 us -> 163 us  [body(): latent_grad = lax.psum(contract_cols(error_all, decoder), ('mp', 'tok'))]
where the time goes in v1:
time: 759 us; the launch traced here: 758 us
  waiting for transfers between devices  392 us (52%)
  blocking collectives  277 us (36%)
  starting transfers between devices  56.6 us (7%)
  between operations  14.9 us (2%)
  local copies, waits for them, and re-layouts  10.1 us (1%)
    psum x1, waiting for transfers between devices, body(): pre = lax.psum(partial_pre, ('mp', 'tok'))  180 us
    psum x1, waiting for transfers between devices, body(): latent_grad = lax.psum(contract_cols(error_all, decoder), ('mp', 'tok'))  163 us
    unnamed x2, blocking collectives  118 us
    all_gather x1, blocking collectives, body(): gathered = lax.all_gather(x_rows, 'lat', axis=0, tiled=True)  61.9 us
    unnamed x16, starting transfers between devices  56.5 us
    all_gather x1, blocking collectives, body(): acts_all = lax.all_gather(acts, 'lat', axis=0, tiled=True)  49.4 us
    reduce_scatter x1, waiting for transfers between devices, body(): lax.psum_scatter(jnp.concatenate([jnp.dot(block, gate_local, preferred_el...  47.7 us
    all_to_all x1, blocking collectives, body(): lax.all_to_all(jnp.stack([unit for _ in range(lax.axis_size('lat'))]), ax...  32.4 us
  transfers between devices with their start and end apart: 19, of which 4 were waited for; matrix products, arithmetic and copies ran while one was open for 0% of the time, Pallas kernels for 0%

profile of v1, /device:TPU:1, one launch (start us, length us, event | category | flops | bytes accessed | tf_op | source)
XLA Modules:
  0.0 758.1 jit_solution(1334212710827914043)
XLA Ops:
  7.2 0.8 copy.20
  8.0 61.9 %all-gather = bf16[1,384,576]{2,0,1:T(2,128)(2,1)S(1)} all-gather(bf16[1,12,576]{2,0,1:T(2,128)(2,1)S(1)} %copy.20), channel_id=2, replica_groups=mesh['mp'=2,'tok'=8,'lat'=32] {'lat'}, dimensions={1}, use_global_device_ids=true | all-gather | bytes 456192 | tf_op jit(solution)/shard_map/all_gather | solution.py:21
  70.0 0.7 copy.21
  70.6 0.6 fusion.4
  71.3 0.6 fusion.6
  71.9 0.1 pad_maximum_fusion
  72.1 2.0 copy.25
  74.1 0.0 all-reduce.7.cloned.1.call-start
  74.1 47.7 %reduce-scatter.8.cloned.1.call-done = f32[48,1152]{1,0:T(8,128)} async-done(((f32[384,1152]{1,0:T(8,128)}), f32[48,1152]{1,0:T(8,128)}) %reduce-scatter.8.cloned.1.call-update) | async-done | bytes 221200 | tf_op jit(solution)/shard_map/reduce_scatter | solution.py:26
  121.8 1.1 fusion.24
  122.9 15.4 %all_gather.10 = bf16[384,576]{1,0:T(8,128)(2,1)S(1)} all-gather(bf16[48,576]{1,0:T(8,128)(2,1)S(1)} %fusion.24), channel_id=1, replica_groups=mesh['mp'=2,'tok'=8,'lat'=32] {'tok'}, dimensions={0}, use_global_device_ids=true | all-gather | bytes 497664 | tf_op jit(solution)/shard_map/all_gather | solution.py:39
  138.2 0.6 fusion.2
  138.8 59.0 %fusion = f32[16,576]{1,0:T(8,128)S(1)} fusion(f32[384,576]{1,0:T(8,128)S(1)} %fusion.2), kind=kCustom, calls=%all-reduce-scatter | all-reduce-scatter fusion | flops 294913 | bytes 923648
  197.9 1.7 collective-permute-start
  199.6 2.1 collective-permute-start.1
  201.7 6.0 collective-permute-start.7
  207.7 4.9 collective-permute-start.2
  212.7 4.9 collective-permute-start.3
  217.6 2.1 collective-permute-start.4
  219.8 3.5 collective-permute-start.5
  223.2 2.8 collective-permute-start.6
  226.1 1.3 dynamic-slice.6
  228.1 1.3 concatenate.4
  229.4 49.4 %all-gather.1 = bf16[32,12,576]{2,1,0:T(8,128)(2,1)S(1)} all-gather(bf16[1,12,576]{2,1,0:T(8,128)(2,1)S(1)} %fusion.30), channel_id=1, replica_groups=mesh['mp'=2,'tok'=8,'lat'=32] {'lat'}, dimensions={0}, use_global_device_ids=true | all-gather | bytes 456192 | tf_op jit(solution)/shard_map/all_gather | solution.py:48
  278.8 0.2 reshape.15
  279.1 1.1 fusion.14
  280.2 0.0 all-reduce.9.cloned.1.call-start
  280.2 180.0 %all-reduce.7.cloned.1.call-done = f32[384,256]{1,0:T(8,128)} async-done(((f32[384,256]{1,0:T(8,128)}), f32[384,256]{1,0:T(8,128)}) %all-reduce.7.cloned.1.call-update) | async-done | bytes 393232 | tf_op jit(solution)/shard_map/psum | solution.py:50
  460.2 1.3 fusion.12
  461.6 59.2 %fusion.1 = f32[16,576]{1,0:T(8,128)S(1)} fusion(f32[384,576]{1,0:T(8,128)S(1)} %fusion.12), kind=kCustom, calls=%all-reduce-scatter.1 | all-reduce-scatter fusion | flops 294913 | bytes 923648
  520.7 1.3 collective-permute-start.10
  522.0 3.4 collective-permute-start.11
  525.5 7.0 collective-permute-start.15
  532.6 4.5 collective-permute-start.12
  537.1 3.9 collective-permute-start.13
  541.0 2.9 collective-permute-start.14
  543.9 3.1 collective-permute-start.8
  547.0 2.2 collective-permute-start.9
  549.3 1.0 collective-permute-done.9
  550.3 1.0 concatenate.5
  551.3 0.1 stack.2
  551.4 32.4 %all_to_all.5 = bf16[32,12,576]{2,1,0:T(8,128)(2,1)S(1)} all-to-all(bf16[32,12,576]{2,1,0:T(8,128)(2,1)S(1)} %stack.2), channel_id=1, replica_groups=mesh['mp'=2,'tok'=8,'lat'=32] {'lat'}, dimensions={0} | all-to-all | bytes 884736 | tf_op jit(solution)/shard_map/all_to_all | solution.py:64
  583.8 0.2 reshape.12
  584.0 1.1 fusion.10
  585.1 0.6 copy.24
  585.8 1.2 convolution_bitcast_fusion
  586.9 162.8 %all-reduce.9.cloned.1.call-done = f32[384,256]{1,0:T(8,128)} async-done(((f32[384,256]{1,0:T(8,128)}), f32[384,256]{1,0:T(8,128)}) %all-reduce.9.cloned.1.call-update) | async-done | bytes 393232 | tf_op jit(solution)/shard_map/psum | solution.py:73
  749.8 1.8 copy.29
  (41 shorter events, 0.2 us)
Async XLA Ops:
  7.2 63.5 %copy-start = (bf16[1,576,576]{2,1,0:T(8,128)(2,1)S(1)}, bf16[1,576,576]{2,1,0:T(8,128)(2,1)}, u32[]{:S(2)}) copy-start(bf16[1,576,576]{2,1,0:T(8,128)(2,1)} %param.10) | copy-start | bytes 1990660
  7.2 114.6 %reduce-scatter.8.cloned.1.call-start = ((), (), s32[]{:S(2)}) async-start(), calls=%async_computation.4 | async-start | bytes 1990656 | tf_op jit(solution)/shard_map/reduce_scatter | solution.py:26
  70.0 1.3 copy-start.3
  74.0 64.2 %copy-start.4 = (bf16[1,576,576]{2,1,0:T(8,128)(2,1)S(1)}, bf16[1,576,576]{2,1,0:T(8,128)(2,1)}, u32[]{:S(2)}) copy-start(bf16[1,576,576]{2,1,0:T(8,128)(2,1)} %param.11) | copy-start | bytes 1990660
  74.1 386.2 %all-reduce.7.cloned.1.call-start = ((), (), s32[]{:S(2)}) async-start(), calls=%async_computation.2 | async-start | bytes 786432 | tf_op jit(solution)/shard_map/psum | solution.py:50
  138.8 140.3 %copy-start.5 = (bf16[1,576,256]{2,1,0:T(8,128)(2,1)S(1)}, bf16[1,576,256]{2,1,0:T(8,128)(2,1)}, u32[]{:S(2)}) copy-start(bf16[1,576,256]{2,1,0:T(8,128)(2,1)} %param.12) | copy-start | bytes 884740
  197.9 21.9 %collective-permute-start = (bf16[16,576]{1,0:T(8,128)(2,1)S(1)}, bf16[16,576]{1,0:T(8,128)(2,1)S(1)}, u32[]{:S(2)}, u32[]{:S(2)}) collective-permute-start(bf16[16,576]{1,0:T(8,128)(2,1)S(1)} %convert.14), channel_id=1, source_target_pairs={{0,1},{1,2},{2,3},{3,4},{4,5},{5,6},{6,7},{7,8},{8,9},{9,10},{10,1... | collective-permute-start | bytes 55304
  199.6 23.6 %collective-permute-start.1 = (bf16[16,576]{1,0:T(8,128)(2,1)S(1)}, bf16[16,576]{1,0:T(8,128)(2,1)S(1)}, u32[]{:S(2)}, u32[]{:S(2)}) collective-permute-start(bf16[16,576]{1,0:T(8,128)(2,1)S(1)} %convert.14), channel_id=1, source_target_pairs={{0,2},{1,3},{2,4},{3,5},{4,6},{5,7},{6,8},{7,9},{8,10},{9,11},{10,... | collective-permute-start | bytes 55304
  201.7 15.9 %collective-permute-start.7 = (bf16[12,576]{1,0:T(8,128)(2,1)S(1)}, bf16[12,576]{1,0:T(8,128)(2,1)S(1)}, u32[]{:S(2)}, u32[]{:S(2)}) collective-permute-start(bf16[12,576]{1,0:T(8,128)(2,1)S(1)} %slice.10), channel_id=1, source_target_pairs={{0,8},{1,9},{2,10},{3,11},{4,12},{5,13},{6,14},{7,15},{8,16},{9,17... | collective-permute-start | bytes 41480
  207.7 20.3 %collective-permute-start.2 = (bf16[16,576]{1,0:T(8,128)(2,1)S(1)}, bf16[16,576]{1,0:T(8,128)(2,1)S(1)}, u32[]{:S(2)}, u32[]{:S(2)}) collective-permute-start(bf16[16,576]{1,0:T(8,128)(2,1)S(1)} %convert.14), channel_id=1, source_target_pairs={{0,3},{1,4},{2,5},{3,6},{4,7},{5,8},{6,9},{7,10},{8,11},{9,12},{10... | collective-permute-start | bytes 55304
  212.7 15.3 %collective-permute-start.3 = (bf16[16,576]{1,0:T(8,128)(2,1)S(1)}, bf16[16,576]{1,0:T(8,128)(2,1)S(1)}, u32[]{:S(2)}, u32[]{:S(2)}) collective-permute-start(bf16[16,576]{1,0:T(8,128)(2,1)S(1)} %convert.14), channel_id=1, source_target_pairs={{0,4},{1,5},{2,6},{3,7},{4,8},{5,9},{6,10},{7,11},{8,12},{9,13},{1... | collective-permute-start | bytes 55304
  217.6 10.4 %collective-permute-start.4 = (bf16[16,576]{1,0:T(8,128)(2,1)S(1)}, bf16[16,576]{1,0:T(8,128)(2,1)S(1)}, u32[]{:S(2)}, u32[]{:S(2)}) collective-permute-start(bf16[16,576]{1,0:T(8,128)(2,1)S(1)} %convert.14), channel_id=1, source_target_pairs={{0,5},{1,6},{2,7},{3,8},{4,9},{5,10},{6,11},{7,12},{8,13},{9,14},{... | collective-permute-start | bytes 55304
  219.8 8.3 %collective-permute-start.5 = (bf16[16,576]{1,0:T(8,128)(2,1)S(1)}, bf16[16,576]{1,0:T(8,128)(2,1)S(1)}, u32[]{:S(2)}, u32[]{:S(2)}) collective-permute-start(bf16[16,576]{1,0:T(8,128)(2,1)S(1)} %convert.14), channel_id=1, source_target_pairs={{0,6},{1,7},{2,8},{3,9},{4,10},{5,11},{6,12},{7,13},{8,14},{9,15},... | collective-permute-start | bytes 55304
  223.2 4.8 collective-permute-start.6
  229.4 230.8 %copy-start.2 = (bf16[256,1,576]{0,2,1:T(8,128)(2,1)S(1)}, bf16[256,1,576]{0,2,1:T(8,128)(2,1)}, u32[]{:S(2)}) copy-start(bf16[256,1,576]{0,2,1:T(8,128)(2,1)} %param.14) | copy-start | bytes 884740
  229.4 230.8 %copy-start.6 = (f32[256]{0:T(256)S(1)}, f32[256]{0:T(256)}, u32[]{:S(2)}) copy-start(f32[256]{0:T(256)} %param.13) | copy-start | bytes 3076
  280.2 269.0 %copy-start.7 = (f32[1,576]{1,0:T(1,128)S(1)}, f32[1,576]{1,0:T(1,128)}, u32[]{:S(2)}) copy-start(f32[1,576]{1,0:T(1,128)} %param.15) | copy-start | bytes 6916
  280.2 469.6 %all-reduce.9.cloned.1.call-start = ((), (), s32[]{:S(2)}) async-start(), calls=%async_computation.3 | async-start | bytes 786432 | tf_op jit(solution)/shard_map/psum | solution.py:73
  520.7 23.1 %collective-permute-start.10 = (f32[16,576]{1,0:T(8,128)S(1)}, f32[16,576]{1,0:T(8,128)S(1)}, u32[]{:S(2)}, u32[]{:S(2)}) collective-permute-start(f32[16,576]{1,0:T(8,128)S(1)} %fusion.1), channel_id=1, source_target_pairs={{0,3},{1,4},{2,5},{3,6},{4,7},{5,8},{6,9},{7,10},{8,11},{9,12},{10... | collective-permute-start | bytes 110600
  522.0 24.9 %collective-permute-start.11 = (f32[16,576]{1,0:T(8,128)S(1)}, f32[16,576]{1,0:T(8,128)S(1)}, u32[]{:S(2)}, u32[]{:S(2)}) collective-permute-start(f32[16,576]{1,0:T(8,128)S(1)} %fusion.1), channel_id=1, source_target_pairs={{0,4},{1,5},{2,6},{3,7},{4,8},{5,9},{6,10},{7,11},{8,12},{9,13},{1... | collective-permute-start | bytes 110600
  525.5 15.5 %collective-permute-start.15 = (f32[12,576]{1,0:T(8,128)S(1)}, f32[12,576]{1,0:T(8,128)S(1)}, u32[]{:S(2)}, u32[]{:S(2)}) collective-permute-start(f32[12,576]{1,0:T(8,128)S(1)} %slice.11), channel_id=1, source_target_pairs={{0,8},{1,9},{2,10},{3,11},{4,12},{5,13},{6,14},{7,15},{8,16},{9,17... | collective-permute-start | bytes 82952
  532.6 16.7 %collective-permute-start.12 = (f32[16,576]{1,0:T(8,128)S(1)}, f32[16,576]{1,0:T(8,128)S(1)}, u32[]{:S(2)}, u32[]{:S(2)}) collective-permute-start(f32[16,576]{1,0:T(8,128)S(1)} %fusion.1), channel_id=1, source_target_pairs={{0,5},{1,6},{2,7},{3,8},{4,9},{5,10},{6,11},{7,12},{8,13},{9,14},{... | collective-permute-start | bytes 110600
  537.1 12.2 %collective-permute-start.13 = (f32[16,576]{1,0:T(8,128)S(1)}, f32[16,576]{1,0:T(8,128)S(1)}, u32[]{:S(2)}, u32[]{:S(2)}) collective-permute-start(f32[16,576]{1,0:T(8,128)S(1)} %fusion.1), channel_id=1, source_target_pairs={{0,6},{1,7},{2,8},{3,9},{4,10},{5,11},{6,12},{7,13},{8,14},{9,15},... | collective-permute-start | bytes 110600
  541.0 8.2 %collective-permute-start.14 = (f32[16,576]{1,0:T(8,128)S(1)}, f32[16,576]{1,0:T(8,128)S(1)}, u32[]{:S(2)}, u32[]{:S(2)}) collective-permute-start(f32[16,576]{1,0:T(8,128)S(1)} %fusion.1), channel_id=1, source_target_pairs={{0,7},{1,8},{2,9},{3,10},{4,11},{5,12},{6,13},{7,14},{8,15},{9,16}... | collective-permute-start | bytes 110600
  543.9 5.4 collective-permute-start.8
  547.0 3.3 collective-permute-start.9
  551.4 34.4 %copy-start.1 = (f32[384,256]{1,0:T(8,128)S(1)}, f32[384,256]{1,0:T(8,128)}, u32[]{:S(2)}) copy-start(f32[384,256]{1,0:T(8,128)} %all-reduce.7.cloned.1.call-done) | copy-start | bytes 1179652
Sparse Core Ops, SparseCore 0:
  74.2 47.5 reduce-scatter.7
  280.3 179.8 all-reduce.6
  585.2 164.4 all-reduce.8
